TPU v7x, 32 devices: a whole 2x2x4 slice. The times are simulated.
32 devices in a mesh: dp: 2 (over x), row: 4 (over y, core), col: 4 (over z).
Axes of the slice: x: 2, y: 2, z: 4, core: 2. Of those that a mesh axis runs over, the one named last changes fastest.
Arguments:
- tokens: bfloat16 [768, 39200], P('row', ('dp', 'col')), may hold values from -6 to 6
- grad_out: bfloat16 [768, 39200], P('row', ('dp', 'col')), may hold values from -6 to 6
- adapter_index: int32 [8, 1], replicated, may hold values from 0 to 7
- norm1_gain: bfloat16 [768], P('row'), may hold values from 0.099609375 to 1.8984375
- norm2_gain: bfloat16 [768], P('row'), may hold values from 0.099609375 to 1.8984375
- qkv_weight: bfloat16 [768, 2304], P('row', 'col'), may hold values from -0.21875 to 0.21875
- proj_weight: bfloat16 [768, 768], P('col', 'row'), may hold values from -0.875 to 0.875
- fc1_weight: bfloat16 [768, 3072], P('row', 'col'), may hold values from -0.21875 to 0.21875
- fc2_weight: bfloat16 [768, 3072], P('row', 'col'), may hold values from -0.109375 to 0.109375
- rel_h: bfloat16 [27, 64], replicated, may hold values from -0.59765625 to 0.59765625
- rel_w: bfloat16 [27, 64], replicated, may hold values from -0.59765625 to 0.59765625
- qkv_down: bfloat16 [8, 768, 16], P(None, 'row'), may hold values from -0.21875 to 0.21875
- qkv_up: bfloat16 [8, 16, 2304], P(None, None, 'col'), may hold values from -0.75 to 0.75
- proj_down: bfloat16 [8, 768, 16], P(None, 'col'), may hold values from -0.21875 to 0.21875
- proj_up: bfloat16 [8, 16, 768], P(None, None, 'row'), may hold values from -0.75 to 0.75
- fc1_down: bfloat16 [8, 768, 16], P(None, 'row'), may hold values from -0.21875 to 0.21875
- fc1_up: bfloat16 [8, 16, 3072], P(None, None, 'col'), may hold values from -0.75 to 0.75
- fc2_down: bfloat16 [8, 3072, 16], P(None, 'col'), may hold values from -0.109375 to 0.109375
- fc2_up: bfloat16 [8, 16, 768], P(None, None, 'row'), may hold values from -0.75 to 0.75
Outputs:
- out: bfloat16 [768, 39200], P('row', ('dp', 'col'))
- tokens_grad: float32 [768, 39200], P('row', ('dp', 'col'))
- qkv_down_grad: float32 [8, 768, 16], P(None, 'row')
- qkv_up_grad: float32 [8, 16, 2304], P(None, None, 'col')
- proj_down_grad: float32 [8, 768, 16], P(None, 'col')
- proj_up_grad: float32 [8, 16, 768], P(None, None, 'row')
- fc1_down_grad: float32 [8, 768, 16], P(None, 'row')
- fc1_up_grad: float32 [8, 16, 3072], P(None, None, 'col')
- fc2_down_grad: float32 [8, 3072, 16], P(None, 'col')
- fc2_up_grad: float32 [8, 16, 768], P(None, None, 'row')
Inputs may be any that keep to these rules, and one draw needn't show every extreme that they name: `adapter_index`: every one of the 8 adapters is chosen by at least one image.
All inputs are finite; a program needn't handle non-finite values.
Results may differ from a plain program's by a relative error of at most 0.015.
Values may be sent and summed in bfloat16 or wider, within the bound.
No kernel may reach another device: no remote copies, remote signals or barrier semaphores. Data moves between devices by JAX's collectives and lax.ppermute only.
A program may use at most 448 MiB of HBM per device.

v0:
```python
import jax
import jax.numpy as jnp
from jax import lax
from jax.sharding import PartitionSpec as P

D = 768
HD = 64
WIN = 14
SIDE = 64
ADAPT = 8
NWIN_SIDE = 5
IMG_TOK = 4900
PRECISE = lax.Precision.HIGHEST
EPSILON = 1e-06


def exact_gelu(values):
    return jax.nn.gelu(values, approximate=False)


def valid_rows():
    position = jnp.arange(IMG_TOK, dtype=jnp.int32)
    window = position // (WIN * WIN)
    inside = position % (WIN * WIN)
    image_row = window // NWIN_SIDE * WIN + inside // WIN
    image_col = window % NWIN_SIDE * WIN + inside % WIN
    return ((image_row < SIDE) & (image_col < SIDE)).astype(jnp.float32)


def rel_table(rel_param):
    offsets = (
        jnp.arange(WIN, dtype=jnp.int32)[:, None]
        - jnp.arange(WIN, dtype=jnp.int32)[None, :]
        + WIN
        - 1
    )
    one_hot = (
        offsets[:, :, None] == jnp.arange(2 * WIN - 1, dtype=jnp.int32)[None, None, :]
    ).astype(jnp.bfloat16)
    return jnp.einsum("akn,nc->akc", one_hot, rel_param, preferred_element_type=jnp.float32).astype(
        jnp.bfloat16
    )


def pick_one(adapter, own_pick):
    return jnp.einsum("a,ade->de", own_pick, adapter.astype(jnp.float32), precision=PRECISE).astype(
        jnp.bfloat16
    )


def row_totals(first_sum, second_sum):
    return lax.psum((first_sum, second_sum), "row")


def norm_forward(values):
    totals = row_totals(jnp.sum(values, axis=1), jnp.sum(values * values, axis=1))
    center = totals[0] / D
    inv_std = lax.rsqrt(totals[1] / D - center * center + EPSILON)
    return ((values - center[:, None]) * inv_std[:, None], inv_std)


def norm_backward(grad_normed, normed, inv_std):
    totals = row_totals(jnp.sum(grad_normed, axis=1), jnp.sum(grad_normed * normed, axis=1))
    return inv_std[:, None] * (
        grad_normed - totals[0][:, None] / D - normed * totals[1][:, None] / D
    )


def local_norm(values):
    center = jnp.sum(values, axis=1) / D
    inv_std = lax.rsqrt(jnp.sum(values * values, axis=1) / D - center * center + EPSILON)
    return ((values - center[:, None]) * inv_std[:, None], inv_std)


def local_norm_back(grad_normed, normed, inv_std):
    first_mean = jnp.sum(grad_normed, axis=1) / D
    second_mean = jnp.sum(grad_normed * normed, axis=1) / D
    return inv_std[:, None] * (grad_normed - first_mean[:, None] - normed * second_mean[:, None])


def to_features(values):
    return lax.all_to_all(
        values.astype(jnp.bfloat16), "row", split_axis=0, concat_axis=1, tiled=True
    ).astype(values.dtype)


def to_tokens(values):
    return lax.all_to_all(
        values.astype(jnp.bfloat16), "row", split_axis=1, concat_axis=0, tiled=True
    ).astype(values.dtype)


def token_rows(values):
    return lax.all_to_all(values, "row", split_axis=0, concat_axis=1, tiled=True)


def head_cols(values):
    return lax.all_to_all(values, "row", split_axis=1, concat_axis=0, tiled=True)


def head_sums(values):
    return lax.all_to_all(
        values.astype(jnp.bfloat16), "row", split_axis=1, concat_axis=0, tiled=True
    ).astype(values.dtype)


def adapted_local(inputs, weight, down_mat, up_mat):
    product = jnp.dot(inputs, weight, preferred_element_type=jnp.float32)
    reduced = jnp.dot(inputs, down_mat, preferred_element_type=jnp.float32)
    return product + jnp.dot(reduced, up_mat.astype(jnp.float32), precision=PRECISE)


def adapted_back(grads, weight, down_mat, up_mat):
    contract = (((1,), (1,)), ((), ()))
    product = lax.dot_general(grads, weight, contract, preferred_element_type=jnp.float32)
    reduced = lax.dot_general(grads, up_mat, contract, preferred_element_type=jnp.float32)
    return product + lax.dot_general(
        reduced, down_mat.astype(jnp.float32), contract, precision=PRECISE
    )


def pair_grads(inputs_m, grads_m, down_m, up_m):
    reduced = jnp.dot(inputs_m, down_m, preferred_element_type=jnp.float32)
    back_red = lax.dot_general(
        grads_m, up_m, (((1,), (1,)), ((), ())), preferred_element_type=jnp.float32
    )
    grad_down = jnp.einsum("td,tr->dr", inputs_m, back_red, precision=PRECISE)
    grad_up = jnp.einsum("tr,to->ro", reduced, grads_m, precision=PRECISE)
    return (grad_down, grad_up)


def spread_pick(own_pick, grad_mat):
    return jnp.einsum("a,de->ade", own_pick, grad_mat)


def take_block(full, dim, index, length):
    return lax.dynamic_slice_in_dim(full, index * length, length, dim)


def split_qkv(qkv_low):
    heads_local = qkv_low.shape[1] // (3 * HD)
    arranged = qkv_low.reshape(NWIN_SIDE * NWIN_SIDE, WIN * WIN, heads_local, 3, HD)
    return (arranged[:, :, :, 0], arranged[:, :, :, 1], arranged[:, :, :, 2])


def score_matrix(query_b, key_b, tables):
    windows = query_b.shape[0]
    heads_local = query_b.shape[2]
    dot_scores = jnp.einsum(
        "nqhc,nkhc->nhqk", query_b, key_b, preferred_element_type=jnp.float32
    ) * HD ** (-0.5)
    spatial = query_b.reshape(windows, WIN, WIN, heads_local, HD)
    rel_rows = jnp.einsum(
        "nabhc,akc->nhabk", spatial, tables[0], preferred_element_type=jnp.float32
    )
    rel_cols = jnp.einsum(
        "nabhc,bkc->nhabk", spatial, tables[1], preferred_element_type=jnp.float32
    )
    shaped = dot_scores.reshape(windows, heads_local, WIN, WIN, WIN, WIN)
    shaped = shaped + rel_rows[:, :, :, :, :, None] + rel_cols[:, :, :, :, None, :]
    return shaped.reshape(windows, heads_local, WIN * WIN, WIN * WIN)


def attend(qkv_low, tables):
    query_b, key_b, value_b = split_qkv(qkv_low)
    scores = score_matrix(query_b, key_b, tables)
    maxima = jnp.max(scores, axis=3, keepdims=True)
    exponent = jnp.exp(scores - maxima)
    sum_exp = jnp.sum(exponent, axis=3, keepdims=True)
    attn_prob = (exponent / sum_exp).astype(jnp.bfloat16)
    attended = jnp.einsum("nhqk,nkhc->nqhc", attn_prob, value_b, preferred_element_type=jnp.float32)
    log_total = (maxima + jnp.log(sum_exp))[:, :, :, 0]
    return (attended.reshape(IMG_TOK, attended.shape[2] * HD).astype(jnp.bfloat16), log_total)


def attend_back(qkv_low, log_total, grad_attended, tables):
    query_b, key_b, value_b = split_qkv(qkv_low)
    windows = query_b.shape[0]
    heads_local = query_b.shape[2]
    scores = score_matrix(query_b, key_b, tables)
    attn_exact = jnp.exp(scores - log_total[:, :, :, None])
    prob_low = attn_exact.astype(jnp.bfloat16)
    grad_o = grad_attended.reshape(windows, WIN * WIN, heads_local, HD)
    grad_v = jnp.einsum("nhqk,nqhc->nkhc", prob_low, grad_o, preferred_element_type=jnp.float32)
    grad_p = jnp.einsum("nqhc,nkhc->nhqk", grad_o, value_b, preferred_element_type=jnp.float32)
    centre = jnp.sum(grad_p * attn_exact, axis=3, keepdims=True)
    grad_s = (attn_exact * (grad_p - centre)).astype(jnp.bfloat16)
    grad_q = jnp.einsum(
        "nhqk,nkhc->nqhc", grad_s, key_b, preferred_element_type=jnp.float32
    ) * HD ** (-0.5)
    grad_k = jnp.einsum(
        "nhqk,nqhc->nkhc", grad_s, query_b, preferred_element_type=jnp.float32
    ) * HD ** (-0.5)
    split_grad = grad_s.astype(jnp.float32).reshape(windows, heads_local, WIN, WIN, WIN, WIN)
    along_rows = jnp.sum(split_grad, axis=5)
    along_cols = jnp.sum(split_grad, axis=4)
    rel_grad = jnp.einsum(
        "nhabk,akc->nabhc", along_rows, tables[0].astype(jnp.float32), precision=PRECISE
    )
    rel_grad = rel_grad + jnp.einsum(
        "nhabk,bkc->nabhc", along_cols, tables[1].astype(jnp.float32), precision=PRECISE
    )
    grad_q = grad_q + rel_grad.reshape(windows, WIN * WIN, heads_local, HD)
    stacked = jnp.stack([grad_q, grad_k, grad_v], axis=3)
    return stacked.reshape(IMG_TOK, heads_local * 3 * HD).astype(jnp.bfloat16)


def body(
    tokens,
    grad_out,
    adapter_index,
    norm1_gain,
    norm2_gain,
    qkv_weight,
    proj_weight,
    fc1_weight,
    fc2_weight,
    rel_h,
    rel_w,
    qkv_down,
    qkv_up,
    proj_down,
    proj_up,
    fc1_down,
    fc1_up,
    fc2_down,
    fc2_up,
):
    members = lax.axis_size("col")
    row_index = lax.axis_index("row")
    col_index = lax.axis_index("col")
    group_ids = lax.dynamic_slice_in_dim(
        adapter_index[:, 0], lax.axis_index("dp") * members, members, 0
    )
    chosen = (group_ids[:, None] == jnp.arange(ADAPT, dtype=jnp.int32)[None, :]).astype(jnp.float32)
    own_pick = chosen[col_index]
    validity = valid_rows()[:, None]
    tables = (rel_table(rel_h), rel_table(rel_w))
    inputs = tokens.astype(jnp.float32).T
    normed_one, inv_one = norm_forward(inputs)
    gain_one = norm1_gain.astype(jnp.float32)
    hidden_one = (normed_one * gain_one * validity).astype(jnp.bfloat16)
    qkv_part, proj_part, qkv_dn_part, proj_up_part = (
        lax.all_gather(qkv_weight, "row", axis=0, tiled=True),
        lax.all_gather(proj_weight, "row", axis=1, tiled=True),
        lax.all_gather(qkv_down, "row", axis=1, tiled=True),
        lax.all_gather(proj_up, "row", axis=2, tiled=True),
    )
    qkv_full, proj_full, qkv_up_all, proj_dn_all = (
        lax.all_gather(qkv_part, "col", axis=1, tiled=True),
        lax.all_gather(proj_part, "col", axis=0, tiled=True),
        lax.all_gather(qkv_up, "col", axis=2, tiled=True),
        lax.all_gather(proj_down, "col", axis=1, tiled=True),
    )
    qkv_dn = pick_one(qkv_dn_part, own_pick)
    qkv_upm = pick_one(qkv_up_all, own_pick)
    proj_dn = pick_one(proj_dn_all, own_pick)
    proj_upm = pick_one(proj_up_part, own_pick)
    hidden_rows = token_rows(hidden_one)
    qkv_rows_out = adapted_local(hidden_rows, qkv_full, qkv_dn, qkv_upm).astype(jnp.bfloat16)
    qkv_low = head_cols(qkv_rows_out)
    attended, log_total = attend(qkv_low, tables)
    attended_rows = token_rows(attended)
    branch = head_sums(adapted_local(attended_rows, proj_full, proj_dn, proj_upm))
    middle = inputs + branch
    grad_final = grad_out.astype(jnp.float32).T * validity
    weight_up, weight_stored, down_one, up_two, gain_full = (
        lax.all_gather(fc1_weight, "row", axis=0, tiled=True),
        lax.all_gather(fc2_weight, "row", axis=0, tiled=True),
        lax.all_gather(fc1_down, "row", axis=1, tiled=True),
        lax.all_gather(fc2_up, "row", axis=2, tiled=True),
        lax.all_gather(norm2_gain, "row", axis=0, tiled=True),
    )
    weight_up, weight_stored, up_one, down_two = (
        lax.all_gather(weight_up, "col", axis=1, tiled=True),
        lax.all_gather(weight_stored, "col", axis=1, tiled=True),
        lax.all_gather(fc1_up, "col", axis=2, tiled=True),
        lax.all_gather(fc2_down, "col", axis=1, tiled=True),
    )
    weight_down = weight_stored.T
    down_fc1 = pick_one(down_one, own_pick)
    up_fc1 = pick_one(up_one, own_pick)
    down_fc2 = pick_one(down_two, own_pick)
    up_fc2 = pick_one(up_two, own_pick)
    local_mid = to_features(middle)
    normed_two, inv_two = local_norm(local_mid)
    gain_two = gain_full.astype(jnp.float32)
    hidden_two = (normed_two * gain_two).astype(jnp.bfloat16)
    pre_act = adapted_local(hidden_two, weight_up, down_fc1, up_fc1)
    activated = exact_gelu(pre_act).astype(jnp.bfloat16)
    mlp_out = to_tokens(adapted_local(activated, weight_down, down_fc2, up_fc2))
    grad_local = to_features(grad_final).astype(jnp.bfloat16)
    grad_activ = adapted_back(grad_local, weight_down, down_fc2, up_fc2)
    gelu_value, gelu_back = jax.vjp(exact_gelu, pre_act)
    grad_pre = gelu_back(grad_activ)[0].astype(jnp.bfloat16)
    grad_hidden_two = adapted_back(grad_pre, weight_up, down_fc1, up_fc1)
    grad_middle = grad_final + to_tokens(
        local_norm_back(grad_hidden_two * gain_two, normed_two, inv_two)
    )
    fc1_local = pair_grads(hidden_two, grad_pre, down_fc1, up_fc1)
    fc2_local = pair_grads(activated, grad_local, down_fc2, up_fc2)
    summed_all = lax.psum(
        (
            spread_pick(own_pick, fc1_local[0]),
            spread_pick(own_pick, fc1_local[1]),
            spread_pick(own_pick, fc2_local[0]),
            spread_pick(own_pick, fc2_local[1]),
        ),
        ("dp", "row", "col"),
    )
    fc1_down_grad = take_block(summed_all[0], 1, row_index, fc1_down.shape[1])
    fc1_up_grad = take_block(summed_all[1], 2, col_index, fc1_up.shape[2])
    fc2_down_grad = take_block(summed_all[2], 1, col_index, fc2_down.shape[1])
    fc2_up_grad = take_block(summed_all[3], 2, row_index, fc2_up.shape[2])
    result = ((middle + mlp_out) * validity).astype(jnp.bfloat16).T
    grad_branch = grad_middle.astype(jnp.bfloat16)
    grad_branch_rows = token_rows(grad_branch)
    grad_attended = head_cols(
        adapted_back(grad_branch_rows, proj_full, proj_dn, proj_upm).astype(jnp.bfloat16)
    )
    grad_qkv = attend_back(qkv_low, log_total, grad_attended, tables)
    grad_qkv_rows = token_rows(grad_qkv)
    grad_hidden_one = head_sums(adapted_back(grad_qkv_rows, qkv_full, qkv_dn, qkv_upm))
    qkv_pair = pair_grads(hidden_rows, grad_qkv_rows, qkv_dn, qkv_upm)
    proj_pair = pair_grads(attended_rows, grad_branch_rows, proj_dn, proj_upm)
    attn_sums = lax.psum(
        (
            spread_pick(own_pick, qkv_pair[0]),
            spread_pick(own_pick, qkv_pair[1]),
            spread_pick(own_pick, proj_pair[0]),
            spread_pick(own_pick, proj_pair[1]),
        ),
        ("dp", "row", "col"),
    )
    qkv_down_grad = take_block(attn_sums[0], 1, row_index, qkv_down.shape[1])
    qkv_up_grad = take_block(attn_sums[1], 2, col_index, qkv_up.shape[2])
    proj_down_grad = take_block(attn_sums[2], 1, col_index, proj_down.shape[1])
    proj_up_grad = take_block(attn_sums[3], 2, row_index, proj_up.shape[2])
    grad_inputs = (
        grad_middle + norm_backward(grad_hidden_one * validity * gain_one, normed_one, inv_one)
    ).T
    return (
        result,
        grad_inputs,
        qkv_down_grad,
        qkv_up_grad,
        proj_down_grad,
        proj_up_grad,
        fc1_down_grad,
        fc1_up_grad,
        fc2_down_grad,
        fc2_up_grad,
    )


def solution(mesh):
    return jax.shard_map(
        body,
        mesh=mesh,
        in_specs=(
            P("row", ("dp", "col")),
            P("row", ("dp", "col")),
            P(),
            P("row"),
            P("row"),
            P("row", "col"),
            P("col", "row"),
            P("row", "col"),
            P("row", "col"),
            P(),
            P(),
            P(None, "row", None),
            P(None, None, "col"),
            P(None, "col", None),
            P(None, None, "row"),
            P(None, "row", None),
            P(None, None, "col"),
            P(None, "col", None),
            P(None, None, "row"),
        ),
        out_specs=(
            P("row", ("dp", "col")),
            P("row", ("dp", "col")),
            P(None, "row", None),
            P(None, None, "col"),
            P(None, "col", None),
            P(None, None, "row"),
            P(None, "row", None),
            P(None, None, "col"),
            P(None, "col", None),
            P(None, None, "row"),
        ),
        check_vma=False,
    )
```

profile of v0, /device:TPU:0, one launch (start us, length us, event | category | flops | bytes accessed | tf_op | source)
XLA Modules:
  0.0 1826.9 jit_solution(15166732212104624496)
XLA Ops:
  46.7 118.0 %all_gather.54 = bf16[8,16,2304]{1,0,2:T(8,128)(2,1)} all-gather(bf16[8,16,576]{1,0,2:T(8,128)(2,1)S(1)} %copy.225), channel_id=1, replica_groups=mesh['dp'=2,'row'=4,'col'=4] {'col'}, dimensions={2}, use_global_device_ids=true | all-gather | bytes 737280 | tf_op jit(solution)/shard_map/all_gather | solution.py:252
  171.6 12.9 all_gather.62
  184.5 30.9 %all_gather.57 = bf16[8,768,16]{2,0,1:T(8,128)(2,1)S(1)} all-gather(bf16[8,192,16]{2,0,1:T(8,128)(2,1)} %copy.243), channel_id=1, replica_groups=mesh['dp'=2,'row'=4,'col'=4] {'col'}, dimensions={1}, use_global_device_ids=true | all-gather | bytes 245760 | tf_op jit(solution)/shard_map/all_gather | solution.py:253
  215.4 12.6 all_gather.53
  263.0 74.5 %all_gather.55 = bf16[192,768]{0,1:T(8,128)(2,1)S(1)} all-gather(bf16[192,192]{0,1:T(8,128)(2,1)S(1)} %copy.241), channel_id=1, replica_groups=mesh['dp'=2,'row'=4,'col'=4] {'row'}, dimensions={1}, use_global_device_ids=true | all-gather | bytes 368640 | tf_op jit(solution)/shard_map/all_gather | solution.py:245
  338.7 13.0 all_gather.58
  372.0 26.8 %reshape.211 = bf16[25,196,3,3,64]{1,0,4,3,2:T(8,128)(2,1)} reshape(bf16[4,1225,576]{1,0,2:T(4,128)(2,1)} %copy.227) | data formatting | bytes 11289600 | tf_op jit(solution)/shard_map/reshape | solution.py:142
  427.1 21.4 %add.271 = f32[25,3,14,14,14,14]{0,5,4,3,2,1:T(8,128)} broadcast(f32[25,3,14,14,14]{0,4,3,2,1:T(8,128)S(1)} %copy.236), dimensions={0,1,2,3,5} | broadcast | bytes 12348000 | tf_op jit(solution)/shard_map/add | solution.py:160
  448.6 64.5 %add.272 = f32[25,3,196,196]{0,3,2,1:T(8,128)} reshape(f32[25,3,14,14,14,14]{0,5,4,3,2,1:T(8,128)} %add.271) | data formatting | bytes 23049600 | tf_op jit(solution)/shard_map/add | solution.py:160
  513.1 39.1 %copy.237 = f32[25,3,196,196]{2,3,1,0:T(8,128)} copy(f32[25,3,196,196]{0,3,2,1:T(8,128)} %add.272) | data formatting | bytes 23049600 | tf_op jit(solution)/shard_map/add | solution.py:160
  563.4 22.8 %add.268 = f32[25,3,14,14,14,14]{0,5,4,3,2,1:T(8,128)} broadcast(f32[25,3,14,14,14]{0,4,3,2,1:T(8,128)} %copy.233), dimensions={0,1,2,3,4} | broadcast | bytes 12348000 | tf_op jit(solution)/shard_map/add | solution.py:160
  586.3 64.5 %add.269 = f32[25,3,196,196]{0,3,2,1:T(8,128)} reshape(f32[25,3,14,14,14,14]{0,5,4,3,2,1:T(8,128)} %add.268) | data formatting | bytes 23049600 | tf_op jit(solution)/shard_map/add | solution.py:160
  650.8 39.1 %copy.234 = f32[25,3,196,196]{2,3,1,0:T(8,128)} copy(f32[25,3,196,196]{0,3,2,1:T(8,128)} %add.269) | data formatting | bytes 23049600 | tf_op jit(solution)/shard_map/add | solution.py:160
  689.9 24.5 %fusion.132 = (f32[25,3,196]{2,1,0:T(4,128)S(1)}, f32[25,3,196,196]{2,3,1,0:T(8,128)}) fusion(f32[25,3,196,196]{2,3,1,0:T(8,128)} %copy.237, f32[25,3,196,196]{2,3,1,0:T(8,128)} %copy.234, bf16[25,196,3,1,64]{1,0,4,3,2:T(8,128)(2,1)} %get-tuple-element.37, bf16[25,196,3,1,64]{1,0,4,3,2:T(8,128)(2,1)S(1)} %copy-done.9), kind=kOutput, calls=%fused_computation.234 | convolution fusion | flops 380303744 | bytes 38396400 | tf_op jit(solution)/shard_map/nqhc,nkhc->nhqk/dot_general | solution.py:149
  779.3 33.6 %all_gather.67 = bf16[8,16,768]{1,0,2:T(8,128)(2,1)S(1)} all-gather(bf16[8,16,192]{1,0,2:T(8,128)(2,1)} %copy.250), channel_id=1, replica_groups=mesh['dp'=2,'row'=4,'col'=4] {'row'}, dimensions={2}, use_global_device_ids=true | all-gather | bytes 245760 | tf_op jit(solution)/shard_map/all_gather | solution.py:271
  814.5 19.3 %all_gather.66 = bf16[8,3072,16]{1,2,0:T(8,128)(2,1)S(1)} all-gather(bf16[8,768,16]{1,2,0:T(8,128)(2,1)} %param.36), channel_id=1, replica_groups=mesh['dp'=2,'row'=4,'col'=4] {'col'}, dimensions={1}, use_global_device_ids=true | all-gather | bytes 983040 | tf_op jit(solution)/shard_map/all_gather | solution.py:278
  868.1 30.2 %all_gather.63 = bf16[8,16,3072]{2,1,0:T(8,128)(2,1)S(1)} all-gather(bf16[8,16,768]{2,1,0:T(8,128)(2,1)S(1)} %copy-done.72), channel_id=1, replica_groups=mesh['dp'=2,'row'=4,'col'=4] {'col'}, dimensions={2}, use_global_device_ids=true | all-gather | bytes 983040 | tf_op jit(solution)/shard_map/all_gather | solution.py:277
  928.8 11.8 fusion.137
  940.6 12.5 all-to-all-done.4
  975.9 41.4 %multiply_convert_fusion.1 = (bf16[1225,3072]{1,0:T(8,128)(2,1)}, f32[1225,3072]{1,0:T(8,128)}, f32[1225,3072]{1,0:T(8,128)}) fusion(f32[1225,3072]{1,0:T(8,128)S(1)} %fusion.135, f32[1225,16]{0,1:T(8,128)S(1)} %fusion.149, bf16[1,16,3072]{2,0,1:T(2,128)(2,1)S(1)} %fusion.64), kind=kOutput, calls=%fused_computation.9 | convolution fusion | flops 970905600 | bytes 52861504 | tf_op jit(solution)/shard_map/dot_general | solution.py:110
  1017.3 23.1 %add_convert_fusion = bf16[1225,3072]{1,0:T(8,128)(2,1)} fusion(f32[1225,3072]{1,0:T(8,128)} %get-tuple-element.32, f32[1225,3072]{1,0:T(8,128)} %fusion.137, f32[1225,3072]{1,0:T(8,128)} %get-tuple-element.51, f32[1225,16]{0,1:T(8,128)S(1)} %fusion.116, bf16[1,3072,16]{1,2,0:T(8,128)(2,1)S(1)} %copy.292), kind=kOutput, calls=%fused_computation.8 | convolution fusion | flops 778982400 | bytes 52861504 | tf_op jit(solution)/shard_map/dot_general | solution.py:117
  1062.8 26.9 %all_to_all.186 = bf16[1225,4,192]{0,2,1:T(8,128)(2,1)S(1)} all-to-all(bf16[1225,4,192]{0,2,1:T(8,128)(2,1)S(1)} %bitcast.307), channel_id=1, replica_groups=mesh['dp'=2,'row'=4,'col'=4] {'row'}, dimensions={1} | all-to-all | bytes 3763200 | tf_op jit(solution)/shard_map/all_to_all | solution.py:88
  1114.9 23.5 %all-to-all-done.8 = bf16[4,1225,192]{1,2,0:T(8,128)(2,1)S(1)} async-done(((bf16[4,1225,192]{1,2,0:T(8,128)(2,1)}), bf16[4,1225,192]{1,2,0:T(8,128)(2,1)S(1)}, u32[]{:S(2)}, u32[]{:S(2)}) %all-to-all-start.8) | async-done | bytes 1881632 | tf_op jit(solution)/shard_map/all_to_all | solution.py:94
  1208.2 21.7 %multiply_reduce_fusion = (f32[25,3,196]{2,1,0:T(4,128)S(1)}, f32[25,3,196,196]{2,3,1,0:T(8,128)}) fusion(f32[25,3,196,196]{2,3,1,0:T(8,128)} %get-tuple-element.50, f32[25,3,196]{2,1,0:T(4,128)S(1)} %log_add_fusion, bf16[25,196,3,1,64]{1,0,4,3,2:T(8,128)(2,1)} %get-tuple-element.35, bf16[25,196,3,64]{1,0,3,2:T(8,128)(2,1)S(1)} %reshape.212), kind=kOutput, calls=%fused_computation.2 | convolution fusion | flops 377422528 | bytes 26930400 | tf_op jit(solution)/shard_map/nqhc,nkhc->nhqk/dot_general | solution.py:185
  1249.0 30.3 %copy.261 = f32[25,3,196,196]{0,3,2,1:T(8,128)} copy(bf16[25,3,196,196]{2,3,1,0:T(8,128)(2,1)} %copy-done.2) | data formatting | bytes 17287200 | tf_op jit(solution)/shard_map/reshape | solution.py:194
  1279.4 64.6 %reshape.221 = f32[25,3,14,14,14,14]{0,5,4,3,2,1:T(8,128)} reshape(f32[25,3,196,196]{0,3,2,1:T(8,128)} %copy.261) | data formatting | bytes 23049600 | tf_op jit(solution)/shard_map/reshape | solution.py:194
  1344.0 94.7 %fusion.128 = (f32[25,3,14,14,14]{0,4,3,2,1:T(8,128)}, f32[25,3,14,14,14]{0,4,3,2,1:T(8,128)}) fusion(f32[25,3,14,14,14,14]{0,5,4,3,2,1:T(8,128)} %reshape.221), kind=kLoop, calls=%fused_computation.231 | loop fusion | flops 5350800 | bytes 13171200 | tf_op jit(solution)/shard_map/reduce_sum | solution.py:195
  1494.7 11.8 copy.269
  1506.5 24.2 %convert_element_type.249 = bf16[4,1225,576]{1,0,2:T(4,128)(2,1)} reshape(bf16[25,196,3,3,64]{1,0,4,3,2:T(8,128)(2,1)} %copy.269) | data formatting | bytes 11289600 | tf_op jit(solution)/shard_map/convert_element_type | solution.py:205
  1577.8 31.0 %all-to-all-done.10 = bf16[4,1225,576]{1,2,0:T(8,128)(2,1)} async-done(((bf16[4,1225,576]{1,2,0:T(8,128)(2,1)}), bf16[4,1225,576]{1,2,0:T(8,128)(2,1)}, u32[]{:S(2)}, u32[]{:S(2)}) %all-to-all-start.10) | async-done | bytes 5644832 | tf_op jit(solution)/shard_map/all_to_all | solution.py:94
  1643.2 17.6 all-to-all-done.11
  1699.4 106.6 %all-reduce.6.cloned.1.call-done = (f32[8,768,16]{1,2,0:T(8,128)}, f32[8,16,2304]{2,1,0:T(8,128)}, f32[8,768,16]{1,2,0:T(8,128)}, f32[8,16,768]{2,1,0:T(8,128)},...) async-done(((f32[8,768,16]{1,2,0:T(8,128)}, f32[8,16,2304]{2,1,0:T(8,128)}, f32[8,768,16]{1,2,0:T(8,128)}, ...) | async-done | bytes 6291472 | tf_op jit(solution)/shard_map/psum | solution.py:326
  (386 shorter events, 621.0 us)
Async XLA Ops:
  7.2 354.6 %copy-start = (bf16[27,64]{1,0:T(8,128)(2,1)S(1)}, bf16[27,64]{1,0:T(8,128)(2,1)}, u32[]{:S(2)}) copy-start(bf16[27,64]{1,0:T(8,128)(2,1)} %param.28) | copy-start | bytes 10372
  7.2 225.9 %all-gather.7.cloned.1.call-start = ((), (), s32[]{:S(2)}) async-start(), calls=%async_computation.12 | async-start | bytes 4423680 | tf_op jit(solution)/shard_map/all_gather | solution.py:250
  41.5 191.2 %all-to-all-start = ((bf16[4,1225,192]{1,2,0:T(8,128)(2,1)}), bf16[4,1225,192]{1,2,0:T(8,128)(2,1)S(1)}, u32[]{:S(2)}, u32[]{:S(2)}) async-start(bf16[4,1225,192]{1,2,0:T(8,128)(2,1)} %copy.222), calls=%async_computation | async-start | bytes 3932160 | tf_op jit(solution)/shard_map/all_to_all | solution.py:94
  45.1 119.6 %copy-start.76 = (bf16[8,192,16]{1,2,0:T(8,128)(2,1)S(1)}, bf16[8,192,16]{1,2,0:T(8,128)(2,1)}, u32[]{:S(2)}) copy-start(bf16[8,192,16]{1,2,0:T(8,128)(2,1)} %param.34) | copy-start | bytes 147460
  45.1 317.2 %all-gather.15.cloned.1.call-start = ((), (), s32[]{:S(2)}) async-start(), calls=%async_computation.16 | async-start | bytes 1474560 | tf_op jit(solution)/shard_map/all_gather | solution.py:269
  45.9 119.1 %copy-start.77 = (bf16[8,192,16]{1,2,0:T(8,128)(2,1)S(1)}, bf16[8,192,16]{1,2,0:T(8,128)(2,1)}, u32[]{:S(2)}) copy-start(bf16[8,192,16]{1,2,0:T(8,128)(2,1)} %param.32) | copy-start | bytes 147460
  45.9 120.1 %copy-start.78 = (bf16[8,192,16]{1,2,0:T(8,128)(2,1)S(1)}, bf16[8,192,16]{1,2,0:T(8,128)(2,1)}, u32[]{:S(2)}) copy-start(bf16[8,192,16]{1,2,0:T(8,128)(2,1)} %param.30) | copy-start | bytes 147460
  171.6 56.4 %copy-start.91 = (s32[8,1]{0,1:T(1,128)S(1)}, s32[8,1]{0,1:T(1,128)}, u32[]{:S(2)}) copy-start(s32[8,1]{0,1:T(1,128)} %param.21) | copy-start | bytes 100
  256.5 81.9 %copy-start.79 = (bf16[8,16,192]{2,1,0:T(8,128)(2,1)S(1)}, bf16[8,16,192]{2,1,0:T(8,128)(2,1)}, u32[]{:S(2)}) copy-start(bf16[8,16,192]{2,1,0:T(8,128)(2,1)} %param.33) | copy-start | bytes 147460
  256.5 105.8 %all-to-all-start.1 = ((bf16[1225,4,576]{0,2,1:T(8,128)(2,1)}), bf16[1225,4,576]{0,2,1:T(8,128)(2,1)}, u32[]{:S(2)}, u32[]{:S(2)}) async-start(bf16[1225,4,576]{0,2,1:T(8,128)(2,1)} %bitcast.293), calls=%async_computation.1 | async-start | bytes 11796480 | tf_op jit(solution)/shard_map/all_to_all | solution.py:98
  261.8 91.5 %copy-start.93 = (u32[32]{0:T(128)S(1)}, u32[32]{0:T(128)}, u32[]{:S(2)}) copy-start(u32[32]{0:T(128)} %constant.173) | copy-start | bytes 388
  261.8 92.7 %copy-start.92 = (bf16[192]{0:T(256)(128)(2,1)S(1)}, bf16[192]{0:T(256)(128)(2,1)}, u32[]{:S(2)}) copy-start(bf16[192]{0:T(256)(128)(2,1)} %param.23) | copy-start | bytes 1156
  261.8 100.2 %copy-start.89 = (bf16[27,64]{1,0:T(8,128)(2,1)S(1)}, bf16[27,64]{1,0:T(8,128)(2,1)}, u32[]{:S(2)}) copy-start(bf16[27,64]{1,0:T(8,128)(2,1)} %param.29) | copy-start | bytes 10372
  261.9 572.0 %all-gather.11.cloned.1.call-start = ((), (), s32[]{:S(2)}) async-start(), calls=%async_computation.14 | async-start | bytes 1474560 | tf_op jit(solution)/shard_map/all_gather | solution.py:268
  262.6 571.3 %all-gather.9.cloned.1.call-start = ((), (), s32[]{:S(2)}) async-start(), calls=%async_computation.13 | async-start | bytes 1474560 | tf_op jit(solution)/shard_map/all_gather | solution.py:251
  338.4 590.4 %all-gather.17.cloned.1.call-start = ((), (), s32[]{:S(2)}) async-start(), calls=%async_computation.17 | async-start | bytes 5898240 | tf_op jit(solution)/shard_map/all_gather | solution.py:276
  362.0 190.1 %copy-start.63 = (bf16[14,14,64,1,1]{2,1,4,3,0:T(8,128)(2,1)}, bf16[14,14,64,1,1]{2,1,4,3,0:T(8,128)(2,1)S(1)}, u32[]{:S(2)}) copy-start(bf16[14,14,64,1,1]{2,1,4,3,0:T(8,128)(2,1)S(1)} %fusion.61) | copy-start | bytes 75268
  746.5 27.9 %all-to-all-start.2 = ((bf16[4,1225,192]{1,2,0:T(8,128)(2,1)}), bf16[4,1225,192]{1,2,0:T(8,128)(2,1)S(1)}, u32[]{:S(2)}, u32[]{:S(2)}) async-start(bf16[4,1225,192]{1,2,0:T(8,128)(2,1)} %copy.240), calls=%async_computation.2 | async-start | bytes 3932160 | tf_op jit(solution)/shard_map/all_to_all | solution.py:94
  775.7 70.0 %all-to-all-start.6 = ((bf16[4,1225,192]{1,2,0:T(8,128)(2,1)}), bf16[4,1225,192]{1,2,0:T(8,128)(2,1)S(1)}, u32[]{:S(2)}, u32[]{:S(2)}) async-start(bf16[4,1225,192]{1,2,0:T(8,128)(2,1)} %copy.253), calls=%async_computation.6 | async-start | bytes 3932160 | tf_op jit(solution)/shard_map/all_to_all | solution.py:82
  779.3 188.6 %all-gather.13.cloned.1.call-start = ((), (), s32[]{:S(2)}) async-start(), calls=%async_computation.15 | async-start | bytes 5898240 | tf_op jit(solution)/shard_map/all_gather | solution.py:275
  845.7 53.6 %all-to-all-start.3 = ((bf16[1225,4,192]{0,2,1:T(8,128)(2,1)}), bf16[1225,4,192]{0,2,1:T(8,128)(2,1)}, u32[]{:S(2)}, u32[]{:S(2)}) async-start(bf16[1225,4,192]{0,2,1:T(8,128)(2,1)} %bitcast.305), calls=%async_computation.3 | async-start | bytes 3932160 | tf_op jit(solution)/shard_map/all_to_all | solution.py:102
  867.8 149.5 %copy-start.55 = (bf16[1,3072,16]{1,2,0:T(8,128)(2,1)}, bf16[1,3072,16]{1,2,0:T(8,128)(2,1)S(1)}, u32[]{:S(2)}) copy-start(bf16[1,3072,16]{1,2,0:T(8,128)(2,1)S(1)} %copy.292) | copy-start | bytes 294916
  899.3 118.0 %copy-start.61 = (f32[1225,16]{0,1:T(8,128)}, f32[1225,16]{0,1:T(8,128)S(1)}, u32[]{:S(2)}) copy-start(f32[1225,16]{0,1:T(8,128)S(1)} %fusion.116) | copy-start | bytes 235204
  924.1 29.0 %all-to-all-start.4 = ((bf16[4,1225,192]{1,2,0:T(8,128)(2,1)}), bf16[4,1225,192]{1,2,0:T(8,128)(2,1)}, u32[]{:S(2)}, u32[]{:S(2)}) async-start(bf16[4,1225,192]{1,2,0:T(8,128)(2,1)} %copy.247), calls=%async_computation.4 | async-start | bytes 3932160 | tf_op jit(solution)/shard_map/all_to_all | solution.py:82
  1110.5 27.9 %all-to-all-start.8 = ((bf16[4,1225,192]{1,2,0:T(8,128)(2,1)}), bf16[4,1225,192]{1,2,0:T(8,128)(2,1)S(1)}, u32[]{:S(2)}, u32[]{:S(2)}) async-start(bf16[4,1225,192]{1,2,0:T(8,128)(2,1)} %copy.256), calls=%async_computation.8 | async-start | bytes 3932160 | tf_op jit(solution)/shard_map/all_to_all | solution.py:94
  1149.2 29.3 %all-to-all-start.9 = ((bf16[1225,4,192]{0,2,1:T(8,128)(2,1)}), bf16[1225,4,192]{0,2,1:T(8,128)(2,1)}, u32[]{:S(2)}, u32[]{:S(2)}) async-start(bf16[1225,4,192]{0,2,1:T(8,128)(2,1)} %bitcast.306), calls=%async_computation.9 | async-start | bytes 3932160 | tf_op jit(solution)/shard_map/all_to_all | solution.py:98
  1178.5 358.2 %all-to-all-start.5 = ((bf16[1225,4,192]{0,2,1:T(8,128)(2,1)}), bf16[1225,4,192]{0,2,1:T(8,128)(2,1)}, u32[]{:S(2)}, u32[]{:S(2)}) async-start(bf16[1225,4,192]{0,2,1:T(8,128)(2,1)} %bitcast.38), calls=%async_computation.5 | async-start | bytes 3932160 | tf_op jit(solution)/shard_map/all_to_all | solution.py:88
  1343.9 94.8 %copy-start.66 = (bf16[14,14,64]{2,1,0:T(8,128)(2,1)S(1)}, bf16[14,14,64]{2,1,0:T(8,128)(2,1)}, u32[]{:S(2)}) copy-start(bf16[14,14,64]{2,1,0:T(8,128)(2,1)} %copy-done.65) | copy-start | bytes 75268
  1536.7 72.1 %all-to-all-start.10 = ((bf16[4,1225,576]{1,2,0:T(8,128)(2,1)}), bf16[4,1225,576]{1,2,0:T(8,128)(2,1)}, u32[]{:S(2)}, u32[]{:S(2)}) async-start(bf16[4,1225,576]{1,2,0:T(8,128)(2,1)} %copy.270), calls=%async_computation.10 | async-start | bytes 11796480 | tf_op jit(solution)/shard_map/all_to_all | solution.py:94
  1627.2 33.6 %all-to-all-start.11 = ((bf16[1225,4,192]{0,2,1:T(8,128)(2,1)}), bf16[1225,4,192]{0,2,1:T(8,128)(2,1)}, u32[]{:S(2)}, u32[]{:S(2)}) async-start(bf16[1225,4,192]{0,2,1:T(8,128)(2,1)} %bitcast.304), calls=%async_computation.11 | async-start | bytes 3932160 | tf_op jit(solution)/shard_map/all_to_all | solution.py:102
  1631.8 174.2 %all-reduce.6.cloned.1.call-start = ((), (), s32[]{:S(2)}) async-start(), calls=%async_computation.18 | async-start | bytes 12582912 | tf_op jit(solution)/shard_map/psum | solution.py:326
  1689.6 130.2 %copy-start.1 = (bf16[27,64]{1,0:T(8,128)(2,1)S(1)}, bf16[27,64]{1,0:T(8,128)(2,1)}, u32[]{:S(2)}) copy-start(bf16[27,64]{1,0:T(8,128)(2,1)} %param.28) | copy-start | bytes 10372
  (84 other events, 808.3 us)
Sparse Core Ops, SparseCore 0:
  20.2 108.6 all-gather.6
  130.5 16.0 all-gather.14
  264.3 24.6 all-gather.10
  338.5 29.8 all-gather.8
  369.8 88.5 all-gather.16
  834.0 100.3 all-gather.12
  1643.3 162.6 all-reduce.5
where the time goes:
time: 1840 us; the launch traced here: 1830 us
  local copies, waits for them, and re-layouts  647 us (35%)
  blocking collectives  412 us (22%)
  matrix products  314 us (17%)
  waiting for transfers between devices  211 us (11%)
  other arithmetic  177 us (10%)
  starting transfers between devices  49.4 us (3%)
    add x6, local copies, waits for them, and re-layouts, score_matrix(): shaped + rel_rows[:, :, :, :, :, None] + rel_cols[:, :, :, :, None, :]  251 us
    all_gather x1, blocking collectives, body(): lax.all_gather(qkv_up, 'col', axis=2, tiled=True)  118 us
    psum x1, waiting for transfers between devices, body(): lax.psum((spread_pick(own_pick, qkv_pair[0]), spread_pick(own_pick, qkv_p...  107 us
    reshape x2, local copies, waits for them, and re-layouts, attend_back(): grad_s.astype(jnp.float32).reshape(windows, heads_local, WIN, WIN, WIN, WIN)  94.9 us
    reduce_sum x1, other arithmetic, attend_back(): along_rows = jnp.sum(split_grad, axis=5)  94.7 us
    all_gather x1, blocking collectives, body(): lax.all_gather(proj_weight, 'row', axis=1, tiled=True)  74.5 us
    all_to_all x4, waiting for transfers between devices, token_rows(): lax.all_to_all(values, 'row', split_axis=0, concat_axis=1, tiled=True)  65.1 us
    dot_general x4, matrix products, adapted_local(): jnp.dot(reduced, up_mat.astype(jnp.float32), precision=PRECISE)  53.4 us
  transfers between devices with their start and end apart: 18, of which 7 were waited for; matrix products, arithmetic and copies ran while one was open for 52% of the time, Pallas kernels for 0%

commit v1 on v0

--- a/solution.py
+++ b/solution.py
@@ -324,13 +324,16 @@
     qkv_pair = pair_grads(hidden_rows, grad_qkv_rows, qkv_dn, qkv_upm)
     proj_pair = pair_grads(attended_rows, grad_branch_rows, proj_dn, proj_upm)
     attn_sums = lax.psum(
-        (
-            spread_pick(own_pick, qkv_pair[0]),
-            spread_pick(own_pick, qkv_pair[1]),
-            spread_pick(own_pick, proj_pair[0]),
-            spread_pick(own_pick, proj_pair[1]),
+        lax.psum(
+            (
+                spread_pick(own_pick, qkv_pair[0]),
+                spread_pick(own_pick, qkv_pair[1]),
+                spread_pick(own_pick, proj_pair[0]),
+                spread_pick(own_pick, proj_pair[1]),
+            ),
+            ("row", "col"),
         ),
-        ("dp", "row", "col"),
+        "dp",
     )
     qkv_down_grad = take_block(attn_sums[0], 1, row_index, qkv_down.shape[1])
     qkv_up_grad = take_block(attn_sums[1], 2, col_index, qkv_up.shape[2])

time: 1840 us -> 1960 us (1.065)
  waiting for transfers between devices: 211 us -> 319 us
  blocking collectives: 412 us -> 440 us
    psum x0 -> x2, waiting for transfers between devices: none -> 176 us  [the longest x1 111 us: body(): lax.psum((spread_pick(own_pick, fc1_local[0]), spread_pick(own_pick, fc1_...]
    psum x1, waiting for transfers between devices: 107 us -> 63.1 us  [body(): lax.psum((spread_pick(own_pick, qkv_pair[0]), spread_pick(own_pick, qkv_p...]
    all_to_all x0 -> x1, blocking collectives: none -> 26.9 us  [token_rows(): lax.all_to_all(values, 'row', split_axis=0, concat_axis=1, tiled=True)]
    all_to_all x4 -> x3, waiting for transfers between devices: 65.1 us -> 42.5 us  [token_rows(): lax.all_to_all(values, 'row', split_axis=0, concat_axis=1, tiled=True)]
  transfers between devices with their start and end apart: 18 -> 19, of which waited for: 7 -> 7; matrix products, arithmetic and copies ran while one was open for 52% -> 32% of each run, Pallas kernels for 0% -> 0%
where the time goes in v1:
time: 1960 us; the launch traced here: 1950 us
  local copies, waits for them, and re-layouts  646 us (33%)
  blocking collectives  440 us (22%)
  waiting for transfers between devices  319 us (16%)
  matrix products  311 us (16%)
  other arithmetic  173 us (9%)
  starting transfers between devices  42.9 us (2%)
    add x6, local copies, waits for them, and re-layouts, score_matrix(): shaped + rel_rows[:, :, :, :, :, None] + rel_cols[:, :, :, :, None, :]  252 us
    all_gather x1, blocking collectives, body(): lax.all_gather(qkv_up, 'col', axis=2, tiled=True)  118 us
    psum x1, waiting for transfers between devices, body(): lax.psum((spread_pick(own_pick, fc1_local[0]), spread_pick(own_pick, fc1_...  111 us
    reshape x2, local copies, waits for them, and re-layouts, attend_back(): grad_s.astype(jnp.float32).reshape(windows, heads_local, WIN, WIN, WIN, WIN)  95.1 us
    reduce_sum x1, other arithmetic, attend_back(): along_rows = jnp.sum(split_grad, axis=5)  94.7 us
    all_gather x1, blocking collectives, body(): lax.all_gather(proj_weight, 'row', axis=1, tiled=True)  74.6 us
    psum x1, waiting for transfers between devices, body(): lax.psum(lax.psum((spread_pick(own_pick, qkv_pair[0]), spread_pick(own_pi...  64.1 us
    psum x1, waiting for transfers between devices, body(): lax.psum((spread_pick(own_pick, qkv_pair[0]), spread_pick(own_pick, qkv_p...  63.1 us
  transfers between devices with their start and end apart: 19, of which 7 were waited for; matrix products, arithmetic and copies ran while one was open for 32% of the time, Pallas kernels for 0%

profile of v1, /device:TPU:0, one launch (start us, length us, event | category | flops | bytes accessed | tf_op | source)
XLA Modules:
  0.0 1948.6 jit_solution(17408236589304464791)
XLA Ops:
  46.6 118.0 %all_gather.54 = bf16[8,16,2304]{1,0,2:T(8,128)(2,1)} all-gather(bf16[8,16,576]{1,0,2:T(8,128)(2,1)S(1)} %copy.225), channel_id=1, replica_groups=mesh['dp'=2,'row'=4,'col'=4] {'col'}, dimensions={2}, use_global_device_ids=true | all-gather | bytes 737280 | tf_op jit(solution)/shard_map/all_gather | solution.py:252
  171.6 12.9 all_gather.62
  184.4 30.8 %all_gather.57 = bf16[8,768,16]{2,0,1:T(8,128)(2,1)S(1)} all-gather(bf16[8,192,16]{2,0,1:T(8,128)(2,1)} %copy.243), channel_id=1, replica_groups=mesh['dp'=2,'row'=4,'col'=4] {'col'}, dimensions={1}, use_global_device_ids=true | all-gather | bytes 245760 | tf_op jit(solution)/shard_map/all_gather | solution.py:253
  215.3 12.9 all_gather.53
  263.0 74.6 %all_gather.55 = bf16[192,768]{0,1:T(8,128)(2,1)S(1)} all-gather(bf16[192,192]{0,1:T(8,128)(2,1)S(1)} %copy.241), channel_id=1, replica_groups=mesh['dp'=2,'row'=4,'col'=4] {'row'}, dimensions={1}, use_global_device_ids=true | all-gather | bytes 368640 | tf_op jit(solution)/shard_map/all_gather | solution.py:245
  338.8 13.0 all_gather.58
  372.2 26.8 %reshape.211 = bf16[25,196,3,3,64]{1,0,4,3,2:T(8,128)(2,1)} reshape(bf16[4,1225,576]{1,0,2:T(4,128)(2,1)} %copy.227) | data formatting | bytes 11289600 | tf_op jit(solution)/shard_map/reshape | solution.py:142
  427.1 21.4 %add.279 = f32[25,3,14,14,14,14]{0,5,4,3,2,1:T(8,128)} broadcast(f32[25,3,14,14,14]{0,4,3,2,1:T(8,128)S(1)} %copy.236), dimensions={0,1,2,3,5} | broadcast | bytes 12348000 | tf_op jit(solution)/shard_map/add | solution.py:160
  448.5 64.5 %add.280 = f32[25,3,196,196]{0,3,2,1:T(8,128)} reshape(f32[25,3,14,14,14,14]{0,5,4,3,2,1:T(8,128)} %add.279) | data formatting | bytes 23049600 | tf_op jit(solution)/shard_map/add | solution.py:160
  513.0 39.2 %copy.237 = f32[25,3,196,196]{2,3,1,0:T(8,128)} copy(f32[25,3,196,196]{0,3,2,1:T(8,128)} %add.280) | data formatting | bytes 23049600 | tf_op jit(solution)/shard_map/add | solution.py:160
  563.4 22.8 %add.276 = f32[25,3,14,14,14,14]{0,5,4,3,2,1:T(8,128)} broadcast(f32[25,3,14,14,14]{0,4,3,2,1:T(8,128)} %copy.233), dimensions={0,1,2,3,4} | broadcast | bytes 12348000 | tf_op jit(solution)/shard_map/add | solution.py:160
  586.3 64.5 %add.277 = f32[25,3,196,196]{0,3,2,1:T(8,128)} reshape(f32[25,3,14,14,14,14]{0,5,4,3,2,1:T(8,128)} %add.276) | data formatting | bytes 23049600 | tf_op jit(solution)/shard_map/add | solution.py:160
  650.8 39.1 %copy.234 = f32[25,3,196,196]{2,3,1,0:T(8,128)} copy(f32[25,3,196,196]{0,3,2,1:T(8,128)} %add.277) | data formatting | bytes 23049600 | tf_op jit(solution)/shard_map/add | solution.py:160
  689.9 24.7 %fusion.132 = (f32[25,3,196]{2,1,0:T(4,128)S(1)}, f32[25,3,196,196]{2,3,1,0:T(8,128)}) fusion(f32[25,3,196,196]{2,3,1,0:T(8,128)} %copy.237, f32[25,3,196,196]{2,3,1,0:T(8,128)} %copy.234, bf16[25,196,3,1,64]{1,0,4,3,2:T(8,128)(2,1)} %get-tuple-element.41, bf16[25,196,3,1,64]{1,0,4,3,2:T(8,128)(2,1)S(1)} %copy-done.9), kind=kOutput, calls=%fused_computation.234 | convolution fusion | flops 380303744 | bytes 38396400 | tf_op jit(solution)/shard_map/nqhc,nkhc->nhqk/dot_general | solution.py:149
  779.2 33.6 %all_gather.67 = bf16[8,16,768]{1,0,2:T(8,128)(2,1)S(1)} all-gather(bf16[8,16,192]{1,0,2:T(8,128)(2,1)} %copy.250), channel_id=1, replica_groups=mesh['dp'=2,'row'=4,'col'=4] {'row'}, dimensions={2}, use_global_device_ids=true | all-gather | bytes 245760 | tf_op jit(solution)/shard_map/all_gather | solution.py:271
  814.4 19.3 all_gather.66
  868.2 30.2 %all_gather.63 = bf16[8,16,3072]{2,1,0:T(8,128)(2,1)S(1)} all-gather(bf16[8,16,768]{2,1,0:T(8,128)(2,1)S(1)} %copy-done.74), channel_id=1, replica_groups=mesh['dp'=2,'row'=4,'col'=4] {'col'}, dimensions={2}, use_global_device_ids=true | all-gather | bytes 983040 | tf_op jit(solution)/shard_map/all_gather | solution.py:277
  940.7 12.5 all-to-all-done.4
  976.0 41.4 %multiply_convert_fusion.1 = (bf16[1225,3072]{1,0:T(8,128)(2,1)}, f32[1225,3072]{1,0:T(8,128)}, f32[1225,3072]{1,0:T(8,128)}) fusion(f32[1225,3072]{1,0:T(8,128)S(1)} %fusion.135, f32[1225,16]{0,1:T(8,128)S(1)} %fusion.149, bf16[1,16,3072]{2,0,1:T(2,128)(2,1)S(1)} %fusion.64), kind=kOutput, calls=%fused_computation.9 | convolution fusion | flops 970905600 | bytes 52861504 | tf_op jit(solution)/shard_map/dot_general | solution.py:110
  1017.4 22.8 %add_convert_fusion = bf16[1225,3072]{1,0:T(8,128)(2,1)} fusion(f32[1225,3072]{1,0:T(8,128)} %get-tuple-element.36, f32[1225,3072]{1,0:T(8,128)} %fusion.137, f32[1225,3072]{1,0:T(8,128)} %get-tuple-element.55, f32[1225,16]{0,1:T(8,128)S(1)} %fusion.116, bf16[1,3072,16]{1,2,0:T(8,128)(2,1)S(1)} %copy.292), kind=kOutput, calls=%fused_computation.8 | convolution fusion | flops 778982400 | bytes 52861504 | tf_op jit(solution)/shard_map/dot_general | solution.py:117
  1062.6 27.2 %all_to_all.186 = bf16[1225,4,192]{0,2,1:T(8,128)(2,1)S(1)} all-to-all(bf16[1225,4,192]{0,2,1:T(8,128)(2,1)S(1)} %bitcast.307), channel_id=1, replica_groups=mesh['dp'=2,'row'=4,'col'=4] {'row'}, dimensions={1} | all-to-all | bytes 3763200 | tf_op jit(solution)/shard_map/all_to_all | solution.py:88
  1109.3 26.9 %all_to_all.187 = bf16[4,1225,192]{1,2,0:T(8,128)(2,1)S(1)} all-to-all(bf16[4,1225,192]{1,2,0:T(8,128)(2,1)S(1)} %copy.256), channel_id=1, replica_groups=mesh['dp'=2,'row'=4,'col'=4] {'row'}, dimensions={0} | all-to-all | bytes 3763200 | tf_op jit(solution)/shard_map/all_to_all | solution.py:94
  1146.3 24.2 %all-to-all-done.9 = bf16[1225,4,192]{0,2,1:T(8,128)(2,1)S(1)} async-done(((bf16[1225,4,192]{0,2,1:T(8,128)(2,1)}), bf16[1225,4,192]{0,2,1:T(8,128)(2,1)S(1)}, u32[]{:S(2)}, u32[]{:S(2)}) %all-to-all-start.9) | async-done | bytes 1881632 | tf_op jit(solution)/shard_map/all_to_all | solution.py:98
  1193.7 21.8 %multiply_reduce_fusion = (f32[25,3,196]{2,1,0:T(4,128)S(1)}, f32[25,3,196,196]{2,3,1,0:T(8,128)}) fusion(f32[25,3,196,196]{2,3,1,0:T(8,128)} %get-tuple-element.54, f32[25,3,196]{2,1,0:T(4,128)S(1)} %log_add_fusion, bf16[25,196,3,1,64]{1,0,4,3,2:T(8,128)(2,1)} %get-tuple-element.39, bf16[25,196,3,64]{1,0,3,2:T(8,128)(2,1)S(1)} %reshape.212), kind=kOutput, calls=%fused_computation.2 | convolution fusion | flops 377422528 | bytes 26930400 | tf_op jit(solution)/shard_map/nqhc,nkhc->nhqk/dot_general | solution.py:185
  1234.6 30.4 %copy.261 = f32[25,3,196,196]{0,3,2,1:T(8,128)} copy(bf16[25,3,196,196]{2,3,1,0:T(8,128)(2,1)} %copy-done.2) | data formatting | bytes 17287200 | tf_op jit(solution)/shard_map/reshape | solution.py:194
  1264.9 64.7 %reshape.221 = f32[25,3,14,14,14,14]{0,5,4,3,2,1:T(8,128)} reshape(f32[25,3,196,196]{0,3,2,1:T(8,128)} %copy.261) | data formatting | bytes 23049600 | tf_op jit(solution)/shard_map/reshape | solution.py:194
  1329.7 94.7 %fusion.128 = (f32[25,3,14,14,14]{0,4,3,2,1:T(8,128)}, f32[25,3,14,14,14]{0,4,3,2,1:T(8,128)}) fusion(f32[25,3,14,14,14,14]{0,5,4,3,2,1:T(8,128)} %reshape.221), kind=kLoop, calls=%fused_computation.231 | loop fusion | flops 5350800 | bytes 13171200 | tf_op jit(solution)/shard_map/reduce_sum | solution.py:195
  1492.2 24.3 %convert_element_type.249 = bf16[4,1225,576]{1,0,2:T(4,128)(2,1)} reshape(bf16[25,196,3,3,64]{1,0,4,3,2:T(8,128)(2,1)} %copy.269) | data formatting | bytes 11289600 | tf_op jit(solution)/shard_map/convert_element_type | solution.py:205
  1562.5 32.0 %all-to-all-done.10 = bf16[4,1225,576]{1,2,0:T(8,128)(2,1)} async-done(((bf16[4,1225,576]{1,2,0:T(8,128)(2,1)}), bf16[4,1225,576]{1,2,0:T(8,128)(2,1)}, u32[]{:S(2)}, u32[]{:S(2)}) %all-to-all-start.10) | async-done | bytes 5644832 | tf_op jit(solution)/shard_map/all_to_all | solution.py:94
  1652.8 63.1 %all-reduce.12.cloned.1.call-done = (f32[8,768,16]{1,2,0:T(8,128)}, f32[8,16,2304]{2,1,0:T(8,128)}, f32[8,768,16]{1,2,0:T(8,128)}, f32[8,16,768]{2,1,0:T(8,128)}) async-done(((f32[8,768,16]{1,2,0:T(8,128)}, f32[8,16,2304]{2,1,0:T(8,128)}, f32[8,768,16]{1,2,0:T(8,128)}, f32[8,16,768]{2,1,0:T(8,128)}), (f32[8,768,16]{1,2,0:T(8,128)}, f32[8,16,2304]{2,1,0:T(8,128)}, f32[8,768,16]{1,2,0:T(8,128)}, ...) | async-done | bytes 2359312 | tf_op jit(solution)/shard_map/psum | solution.py:327
  1752.2 111.4 %all-reduce.10.cloned.1.call-done = (f32[8,768,16]{1,2,0:T(8,128)}, f32[8,16,3072]{2,1,0:T(8,128)}, f32[8,3072,16]{1,2,0:T(8,128)}, f32[8,16,768]{2,1,0:T(8,128)}) async-done(((f32[8,768,16]{1,2,0:T(8,128)}, f32[8,16,3072]{2,1,0:T(8,128)}, f32[8,3072,16]{1,2,0:T(8,128)}, f32[8,16,768]{2,1,0:T(8,128)}), (f32[8,768,16]{1,2,0:T(8,128)}, f32[8,16,3072]{2,1,0:T(8,128)}, f32[8,3072,16]{1,2,0:T(8,128)}, ...) | async-done | bytes 3932176 | tf_op jit(solution)/shard_map/psum | solution.py:302
  1870.6 64.1 %all-reduce.14.cloned.1.call-done = (f32[8,768,16]{1,2,0:T(8,128)}, f32[8,16,2304]{2,1,0:T(8,128)}, f32[8,768,16]{1,2,0:T(8,128)}, f32[8,16,768]{2,1,0:T(8,128)}) async-done(((f32[8,768,16]{1,2,0:T(8,128)}, f32[8,16,2304]{2,1,0:T(8,128)}, f32[8,768,16]{1,2,0:T(8,128)}, f32[8,16,768]{2,1,0:T(8,128)}), (f32[8,768,16]{1,2,0:T(8,128)}, f32[8,16,2304]{2,1,0:T(8,128)}, f32[8,768,16]{1,2,0:T(8,128)}, ...) | async-done | bytes 2359312 | tf_op jit(solution)/shard_map/psum | solution.py:326
  (388 shorter events, 622.3 us)
Async XLA Ops:
  7.2 354.7 %copy-start = (bf16[27,64]{1,0:T(8,128)(2,1)S(1)}, bf16[27,64]{1,0:T(8,128)(2,1)}, u32[]{:S(2)}) copy-start(bf16[27,64]{1,0:T(8,128)(2,1)} %param.28) | copy-start | bytes 10372
  7.2 226.0 %all-gather.7.cloned.1.call-start = ((), (), s32[]{:S(2)}) async-start(), calls=%async_computation.12 | async-start | bytes 4423680 | tf_op jit(solution)/shard_map/all_gather | solution.py:250
  41.4 191.4 %all-to-all-start = ((bf16[4,1225,192]{1,2,0:T(8,128)(2,1)}), bf16[4,1225,192]{1,2,0:T(8,128)(2,1)S(1)}, u32[]{:S(2)}, u32[]{:S(2)}) async-start(bf16[4,1225,192]{1,2,0:T(8,128)(2,1)} %copy.222), calls=%async_computation | async-start | bytes 3932160 | tf_op jit(solution)/shard_map/all_to_all | solution.py:94
  45.0 119.7 %copy-start.77 = (bf16[8,192,16]{1,2,0:T(8,128)(2,1)S(1)}, bf16[8,192,16]{1,2,0:T(8,128)(2,1)}, u32[]{:S(2)}) copy-start(bf16[8,192,16]{1,2,0:T(8,128)(2,1)} %param.34) | copy-start | bytes 147460
  45.0 317.4 %all-gather.15.cloned.1.call-start = ((), (), s32[]{:S(2)}) async-start(), calls=%async_computation.16 | async-start | bytes 1474560 | tf_op jit(solution)/shard_map/all_gather | solution.py:269
  45.8 119.1 %copy-start.78 = (bf16[8,192,16]{1,2,0:T(8,128)(2,1)S(1)}, bf16[8,192,16]{1,2,0:T(8,128)(2,1)}, u32[]{:S(2)}) copy-start(bf16[8,192,16]{1,2,0:T(8,128)(2,1)} %param.32) | copy-start | bytes 147460
  45.8 120.1 %copy-start.79 = (bf16[8,192,16]{1,2,0:T(8,128)(2,1)S(1)}, bf16[8,192,16]{1,2,0:T(8,128)(2,1)}, u32[]{:S(2)}) copy-start(bf16[8,192,16]{1,2,0:T(8,128)(2,1)} %param.30) | copy-start | bytes 147460
  256.6 81.9 %copy-start.80 = (bf16[8,16,192]{2,1,0:T(8,128)(2,1)S(1)}, bf16[8,16,192]{2,1,0:T(8,128)(2,1)}, u32[]{:S(2)}) copy-start(bf16[8,16,192]{2,1,0:T(8,128)(2,1)} %param.33) | copy-start | bytes 147460
  256.6 105.8 %all-to-all-start.1 = ((bf16[1225,4,576]{0,2,1:T(8,128)(2,1)}), bf16[1225,4,576]{0,2,1:T(8,128)(2,1)}, u32[]{:S(2)}, u32[]{:S(2)}) async-start(bf16[1225,4,576]{0,2,1:T(8,128)(2,1)} %bitcast.291), calls=%async_computation.1 | async-start | bytes 11796480 | tf_op jit(solution)/shard_map/all_to_all | solution.py:98
  261.9 91.5 %copy-start.94 = (u32[32]{0:T(128)S(1)}, u32[32]{0:T(128)}, u32[]{:S(2)}) copy-start(u32[32]{0:T(128)} %constant.173) | copy-start | bytes 388
  261.9 92.7 %copy-start.93 = (bf16[192]{0:T(256)(128)(2,1)S(1)}, bf16[192]{0:T(256)(128)(2,1)}, u32[]{:S(2)}) copy-start(bf16[192]{0:T(256)(128)(2,1)} %param.23) | copy-start | bytes 1156
  262.0 100.2 %copy-start.90 = (bf16[27,64]{1,0:T(8,128)(2,1)S(1)}, bf16[27,64]{1,0:T(8,128)(2,1)}, u32[]{:S(2)}) copy-start(bf16[27,64]{1,0:T(8,128)(2,1)} %param.29) | copy-start | bytes 10372
  262.0 571.8 %all-gather.11.cloned.1.call-start = ((), (), s32[]{:S(2)}) async-start(), calls=%async_computation.14 | async-start | bytes 1474560 | tf_op jit(solution)/shard_map/all_gather | solution.py:268
  262.7 571.1 %all-gather.9.cloned.1.call-start = ((), (), s32[]{:S(2)}) async-start(), calls=%async_computation.13 | async-start | bytes 1474560 | tf_op jit(solution)/shard_map/all_gather | solution.py:251
  338.5 590.4 %all-gather.17.cloned.1.call-start = ((), (), s32[]{:S(2)}) async-start(), calls=%async_computation.17 | async-start | bytes 5898240 | tf_op jit(solution)/shard_map/all_gather | solution.py:276
  362.1 190.0 %copy-start.66 = (bf16[14,14,64,1,1]{2,1,4,3,0:T(8,128)(2,1)}, bf16[14,14,64,1,1]{2,1,4,3,0:T(8,128)(2,1)S(1)}, u32[]{:S(2)}) copy-start(bf16[14,14,64,1,1]{2,1,4,3,0:T(8,128)(2,1)S(1)} %fusion.61) | copy-start | bytes 75268
  746.4 27.9 %all-to-all-start.2 = ((bf16[4,1225,192]{1,2,0:T(8,128)(2,1)}), bf16[4,1225,192]{1,2,0:T(8,128)(2,1)S(1)}, u32[]{:S(2)}, u32[]{:S(2)}) async-start(bf16[4,1225,192]{1,2,0:T(8,128)(2,1)} %copy.240), calls=%async_computation.2 | async-start | bytes 3932160 | tf_op jit(solution)/shard_map/all_to_all | solution.py:94
  775.6 70.0 %all-to-all-start.6 = ((bf16[4,1225,192]{1,2,0:T(8,128)(2,1)}), bf16[4,1225,192]{1,2,0:T(8,128)(2,1)S(1)}, u32[]{:S(2)}, u32[]{:S(2)}) async-start(bf16[4,1225,192]{1,2,0:T(8,128)(2,1)} %copy.253), calls=%async_computation.6 | async-start | bytes 3932160 | tf_op jit(solution)/shard_map/all_to_all | solution.py:82
  779.2 188.8 %all-gather.13.cloned.1.call-start = ((), (), s32[]{:S(2)}) async-start(), calls=%async_computation.15 | async-start | bytes 5898240 | tf_op jit(solution)/shard_map/all_gather | solution.py:275
  845.6 53.9 %all-to-all-start.3 = ((bf16[1225,4,192]{0,2,1:T(8,128)(2,1)}), bf16[1225,4,192]{0,2,1:T(8,128)(2,1)}, u32[]{:S(2)}, u32[]{:S(2)}) async-start(bf16[1225,4,192]{0,2,1:T(8,128)(2,1)} %bitcast.304), calls=%async_computation.3 | async-start | bytes 3932160 | tf_op jit(solution)/shard_map/all_to_all | solution.py:102
  868.0 149.4 %copy-start.58 = (bf16[1,3072,16]{1,2,0:T(8,128)(2,1)}, bf16[1,3072,16]{1,2,0:T(8,128)(2,1)S(1)}, u32[]{:S(2)}) copy-start(bf16[1,3072,16]{1,2,0:T(8,128)(2,1)S(1)} %copy.292) | copy-start | bytes 294916
  899.4 117.9 %copy-start.64 = (f32[1225,16]{0,1:T(8,128)}, f32[1225,16]{0,1:T(8,128)S(1)}, u32[]{:S(2)}) copy-start(f32[1225,16]{0,1:T(8,128)S(1)} %fusion.116) | copy-start | bytes 235204
  924.2 29.0 %all-to-all-start.4 = ((bf16[4,1225,192]{1,2,0:T(8,128)(2,1)}), bf16[4,1225,192]{1,2,0:T(8,128)(2,1)}, u32[]{:S(2)}, u32[]{:S(2)}) async-start(bf16[4,1225,192]{1,2,0:T(8,128)(2,1)} %copy.247), calls=%async_computation.4 | async-start | bytes 3932160 | tf_op jit(solution)/shard_map/all_to_all | solution.py:82
  1142.4 28.0 %all-to-all-start.9 = ((bf16[1225,4,192]{0,2,1:T(8,128)(2,1)}), bf16[1225,4,192]{0,2,1:T(8,128)(2,1)S(1)}, u32[]{:S(2)}, u32[]{:S(2)}) async-start(bf16[1225,4,192]{0,2,1:T(8,128)(2,1)} %bitcast.306), calls=%async_computation.9 | async-start | bytes 3932160 | tf_op jit(solution)/shard_map/all_to_all | solution.py:98
  1329.7 94.8 %copy-start.69 = (bf16[14,14,64]{2,1,0:T(8,128)(2,1)S(1)}, bf16[14,14,64]{2,1,0:T(8,128)(2,1)}, u32[]{:S(2)}) copy-start(bf16[14,14,64]{2,1,0:T(8,128)(2,1)} %copy-done.68) | copy-start | bytes 75268
  1522.5 71.9 %all-to-all-start.10 = ((bf16[4,1225,576]{1,2,0:T(8,128)(2,1)}), bf16[4,1225,576]{1,2,0:T(8,128)(2,1)}, u32[]{:S(2)}, u32[]{:S(2)}) async-start(bf16[4,1225,576]{1,2,0:T(8,128)(2,1)} %copy.270), calls=%async_computation.10 | async-start | bytes 11796480 | tf_op jit(solution)/shard_map/all_to_all | solution.py:94
  1594.5 40.9 %all-to-all-start.5 = ((bf16[1225,4,192]{0,2,1:T(8,128)(2,1)}), bf16[1225,4,192]{0,2,1:T(8,128)(2,1)S(1)}, u32[]{:S(2)}, u32[]{:S(2)}) async-start(bf16[1225,4,192]{0,2,1:T(8,128)(2,1)} %bitcast.302), calls=%async_computation.5 | async-start | bytes 3932160 | tf_op jit(solution)/shard_map/all_to_all | solution.py:88
  1598.1 117.9 %all-reduce.12.cloned.1.call-start = ((), (), s32[]{:S(2)}) async-start(), calls=%async_computation.19 | async-start | bytes 4718592 | tf_op jit(solution)/shard_map/psum | solution.py:327
  1613.4 250.2 %all-reduce.10.cloned.1.call-start = ((), (), s32[]{:S(2)}) async-start(), calls=%async_computation.18 | async-start | bytes 7864320 | tf_op jit(solution)/shard_map/psum | solution.py:302
  1636.7 79.3 %all-to-all-start.11 = ((bf16[1225,4,192]{0,2,1:T(8,128)(2,1)}), bf16[1225,4,192]{0,2,1:T(8,128)(2,1)S(1)}, u32[]{:S(2)}, u32[]{:S(2)}) async-start(bf16[1225,4,192]{0,2,1:T(8,128)(2,1)} %bitcast.303), calls=%async_computation.11 | async-start | bytes 3932160 | tf_op jit(solution)/shard_map/all_to_all | solution.py:102
  1640.3 294.4 %all-reduce.14.cloned.1.call-start = ((), (), s32[]{:S(2)}) async-start(), calls=%async_computation.20 | async-start | bytes 4718592 | tf_op jit(solution)/shard_map/psum | solution.py:326
  1742.5 199.1 %copy-start.1 = (bf16[27,64]{1,0:T(8,128)(2,1)S(1)}, bf16[27,64]{1,0:T(8,128)(2,1)}, u32[]{:S(2)}) copy-start(bf16[27,64]{1,0:T(8,128)(2,1)} %param.28) | copy-start | bytes 10372
  (84 other events, 832.7 us)
Sparse Core Ops, SparseCore 0:
  20.2 108.7 all-gather.6
  130.5 16.0 all-gather.14
  264.4 24.7 all-gather.10
  338.6 29.9 all-gather.8
  370.0 88.5 all-gather.16
  833.9 100.4 all-gather.12
  1613.6 102.3 all-reduce.11
  1722.6 141.0 all-reduce.9
  1866.3 68.3 all-reduce.13
